TPU v7x, 128 devices: a whole 4x4x4 slice. The times are simulated.
128 devices in a mesh: grp: 8 (over z_lo, x), blk: 16 (over z_hi, y, core).
Axes of the slice: x: 4, y: 4, z: 4 (z_hi: 2, z_lo: 2; z = z_hi * 2 + z_lo), core: 2. Of those that a mesh axis runs over, the one named last changes fastest.
Arguments:
- feats: bfloat16 [131072, 256], P(('grp', 'blk')), may hold values from -6 to 6
- weight: bfloat16 [256, 256], replicated, may hold values from -0.375 to 0.375
- cotangent: bfloat16 [131072, 256], P(('grp', 'blk')), may hold values from -6 to 6
- labels: int32 [131072], P(('grp', 'blk')), may hold values from -86 to 171
- tile_vals: bfloat16 [8, 16, 16, 32, 128, 128], P('grp', 'blk'), may hold values from -0.0625 to 0.0625
- tile_row: int32 [8, 16, 16, 32], P('grp', 'blk'), may hold values from 0 to 7
- tile_col: int32 [8, 16, 16, 32], P('grp', 'blk'), may hold values from 0 to 7
- tile_count: int32 [8, 16, 16], P('grp', 'blk'), may hold values from 1 to 32, as said below
- hub_vals: bfloat16 [8, 16, 16, 128, 128], P('grp', 'blk'), may hold values from -0.0625 to 0.0625
- hub_col: int32 [8, 16, 16], P('grp', 'blk'), may hold values from 0 to 7
- hub_dest: int32 [8, 16, 16, 1], P(None, 'blk'), may hold values from 0 to 7; in each aligned block of 16 rows (0 to 15, 16 to 31, ..., all dimensions but the last counted through in order) at most 4 rows name the same one
- hub_row: int32 [8, 16, 16], P(None, 'blk'), may hold values from 0 to 7
Outputs:
- layer_out: bfloat16 [131072, 256], P(('grp', 'blk'))
- grad_feats: bfloat16 [131072, 256], P(('grp', 'blk'))
- grad_weight: float32 [256, 256], replicated
Inputs may be any that keep to these rules, and one draw needn't show every extreme that they name: Only the first tile_count slots of a device's list for a source block are used; some device uses all 32. `hub_dest`: at most 4 of the 16 hub tiles of one device name the same group, and exactly 4 in some devices.
All inputs are finite; a program needn't handle non-finite values.
Results may differ from a plain program's by a relative error of at most 0.007.
Values may be sent and summed in bfloat16 or wider, within the bound.
A program may use at most 192 MiB of HBM per device.

v0:
```python
import math
import jax
import jax.numpy as jnp
from jax import lax
from jax.sharding import PartitionSpec as P


def shifted(value, axis, by):
    size = lax.axis_size(axis)
    return lax.ppermute(value, axis, [(i, (i + by) % size) for i in range(size)])


def local(
    feats,
    weight,
    cotangent,
    labels,
    tile_vals,
    tile_row,
    tile_col,
    tile_count,
    hub_vals,
    hub_col,
    hub_dest,
    hub_row,
):
    n_blocks = lax.axis_size("blk")
    n_groups = lax.axis_size("grp")
    my_block = lax.axis_index("blk")
    my_group = lax.axis_index("grp")
    rows_dev = feats.shape[0]
    width = feats.shape[1]
    tile_size = tile_vals.shape[-1]
    row_tiles = rows_dev // tile_size
    slot_count = tile_vals.shape[3]
    hub_count = hub_vals.shape[2]
    capacity = max(2, hub_count // 4)
    highest = lax.Precision.HIGHEST
    dev_vals = tile_vals[0, 0]
    dev_rows = tile_row[0, 0]
    dev_cols = tile_col[0, 0]
    dev_count = tile_count[0, 0]
    tile_range = jnp.arange(row_tiles, dtype=jnp.int32)
    slot_range = jnp.arange(slot_count, dtype=jnp.int32)
    proj = jnp.dot(feats, weight, preferred_element_type=jnp.float32).astype(jnp.bfloat16)
    own_panel = proj.reshape(row_tiles, tile_size, width)

    def block_parts(source):
        blk_vals = lax.dynamic_index_in_dim(dev_vals, source, 0, keepdims=False)
        blk_rows = lax.dynamic_index_in_dim(dev_rows, source, 0, keepdims=False)
        blk_cols = lax.dynamic_index_in_dim(dev_cols, source, 0, keepdims=False)
        blk_count = lax.dynamic_index_in_dim(dev_count, source, 0, keepdims=False)
        live_mask = (slot_range < blk_count).astype(jnp.float32)
        return (blk_vals, blk_rows, blk_cols, live_mask)

    def forward_block(source, panel_now):
        blk_vals, blk_rows, blk_cols, live_mask = block_parts(source)
        picked = jnp.take(panel_now, blk_cols, axis=0)
        product = jnp.einsum("tij,tjf->tif", blk_vals, picked, preferred_element_type=jnp.float32)
        placing = (blk_rows[:, None] == tile_range[None, :]).astype(jnp.float32) * live_mask[
            :, None
        ]
        return jnp.einsum("tr,tif->rif", placing, product, precision=highest)

    def backward_block(target, grad_tiles):
        blk_vals, blk_rows, blk_cols, live_mask = block_parts(target)
        picked = jnp.take(grad_tiles, blk_rows, axis=0)
        product = jnp.einsum("tij,tif->tjf", blk_vals, picked, preferred_element_type=jnp.float32)
        placing = (blk_cols[:, None] == tile_range[None, :]).astype(jnp.float32) * live_mask[
            :, None
        ]
        return jnp.einsum("tr,tjf->rjf", placing, product, precision=highest)

    agg_sum = forward_block(my_block, own_panel)

    def forward_turn(k, carry):
        panel_now, running = carry
        panel_now = shifted(panel_now, "blk", 1)
        source = (my_block - k) % n_blocks
        return (panel_now, running + forward_block(source, panel_now))

    _, agg_sum = lax.fori_loop(1, n_blocks, forward_turn, (own_panel, agg_sum))
    dest_all = hub_dest[:, 0, :, 0]
    hub_rows_all = hub_row[:, 0, :]
    hub_range = jnp.arange(hub_count, dtype=jnp.int32)
    earlier = hub_range[None, :] < hub_range[:, None]
    same_dest = dest_all[:, :, None] == dest_all[:, None, :]
    rank_all = jnp.sum((same_dest & earlier[None, :, :]).astype(jnp.int32), axis=-1)
    my_dest = lax.dynamic_index_in_dim(dest_all, my_group, 0, keepdims=False)
    my_rank = lax.dynamic_index_in_dim(rank_all, my_group, 0, keepdims=False)
    slot_of = my_dest * capacity + my_rank
    send_place = (
        slot_of[:, None] == jnp.arange(n_groups * capacity, dtype=jnp.int32)[None, :]
    ).astype(jnp.float32)
    hub_tiles = hub_vals[0, 0]
    hub_cols = hub_col[0, 0]
    hub_src = jnp.take(own_panel, hub_cols, axis=0)
    hub_part = jnp.einsum("hij,hjf->hif", hub_tiles, hub_src, preferred_element_type=jnp.float32)
    send_buf = jnp.einsum("hs,hif->sif", send_place, hub_part, precision=highest)
    send_buf = send_buf.reshape(n_groups, capacity, tile_size, width)
    received = lax.all_to_all(send_buf, "grp", split_axis=0, concat_axis=0, tiled=True)
    chosen = (dest_all == my_group).astype(jnp.float32)
    slot_hot = (rank_all[..., None] == jnp.arange(capacity, dtype=jnp.int32)).astype(
        jnp.float32
    ) * chosen[..., None]
    row_hot = (hub_rows_all[..., None] == tile_range).astype(jnp.float32)
    routing = jnp.einsum("shc,shr->scr", slot_hot, row_hot, precision=highest)
    agg_sum = agg_sum + jnp.einsum("scr,scif->rif", routing, received, precision=highest)
    agg_rows = agg_sum.reshape(rows_dev, width)
    layer_out = jax.nn.silu(agg_rows).astype(jnp.bfloat16)
    sigmoid_z = jax.nn.sigmoid(agg_rows)
    slope = sigmoid_z * (1.0 + agg_rows * (1.0 - sigmoid_z))
    keep = (labels >= 0).astype(jnp.float32)[:, None]
    grad_agg = (cotangent.astype(jnp.float32) * keep * slope).astype(jnp.bfloat16)
    grad_tiles = grad_agg.reshape(row_tiles, tile_size, width)
    grad_sum = backward_block((my_block + n_blocks - 1) % n_blocks, grad_tiles)

    def backward_turn(k, running):
        running = shifted(running, "blk", 1)
        return running + backward_block((my_block + n_blocks - 1 - k) % n_blocks, grad_tiles)

    grad_sum = lax.fori_loop(1, n_blocks, backward_turn, grad_sum)
    back_send = jnp.einsum(
        "scr,rif->scif",
        routing.astype(jnp.bfloat16),
        grad_tiles,
        preferred_element_type=jnp.float32,
    ).astype(jnp.bfloat16)
    back_recv = lax.all_to_all(back_send, "grp", split_axis=0, concat_axis=0, tiled=True)
    back_flat = back_recv.reshape(n_groups * capacity, tile_size, width)
    own_pick = jnp.einsum(
        "hs,sif->hif",
        send_place.astype(jnp.bfloat16),
        back_flat,
        preferred_element_type=jnp.float32,
    ).astype(jnp.bfloat16)
    hub_back = jnp.einsum("hij,hif->hjf", hub_tiles, own_pick, preferred_element_type=jnp.float32)
    col_hot = (hub_cols[:, None] == tile_range[None, :]).astype(jnp.float32)
    grad_sum = grad_sum + jnp.einsum("hr,hjf->rjf", col_hot, hub_back, precision=highest)
    grad_rows = grad_sum.reshape(rows_dev, width).astype(jnp.bfloat16)
    weight_term = lax.dot_general(
        feats, grad_rows, (((0,), (0,)), ((), ())), preferred_element_type=jnp.float32
    )
    grad_scale = 1.0 / math.sqrt(rows_dev * n_blocks * n_groups)
    grad_weight = lax.psum(weight_term, ("grp", "blk")) * grad_scale
    grad_feats = lax.dot_general(
        grad_rows, weight, (((1,), (1,)), ((), ())), preferred_element_type=jnp.float32
    ).astype(jnp.bfloat16)
    return (layer_out, grad_feats, grad_weight)


def solution(mesh):
    in_specs = (
        P(("grp", "blk"), None),
        P(),
        P(("grp", "blk"), None),
        P(("grp", "blk")),
        P("grp", "blk", None, None, None, None),
        P("grp", "blk", None, None),
        P("grp", "blk", None, None),
        P("grp", "blk", None),
        P("grp", "blk", None, None, None),
        P("grp", "blk", None),
        P(None, "blk", None, None),
        P(None, "blk", None),
    )
    out_specs = (P(("grp", "blk"), None), P(("grp", "blk"), None), P())
    return jax.shard_map(local, mesh=mesh, in_specs=in_specs, out_specs=out_specs, check_vma=False)
```

profile of v0, /device:TPU:1, one launch (start us, length us, event | category | flops | bytes accessed | tf_op | source)
XLA Modules:
  0.0 958.8 jit_solution(11379729683561159299)
XLA Ops:
  51.4 313.8 %while.34 = (s32[]{:T(128)}, bf16[8,128,256]{2,1,0:T(8,128)(2,1)S(1)}, f32[8,128,256]{2,0,1:T(8,128)}, s32[]{:T(128)}, s32[16,32]{1,0:T(8,128)}, /*index=5*/s32[...) while((s32[]{:T(128)}, ...), condition=%wide.region_1.3_spmd.clone, body=%wide.region_0.2_spmd.clone.sunk | while | flops 370411264 | bytes 29365836 | solution.py:82
  73.1 11.3 %collective-permute-done = bf16[8,128,256]{2,1,0:T(8,128)(2,1)S(1)} collective-permute-done((bf16[8,128,256]{2,1,0:T(8,128)(2,1)S(1)}, bf16[8,128,256]{2,1,0:T(8,128)(2,1)S(1)}, u32[]{:S(2)}, u32[]{:S(2)}) %collective-permute-start) | collective-permute-done | bytes 524320 | tf_op jit(solution)/shard_map/while/body/eval_jaxpr/ppermute | solution.py:10
  95.4 14.3 %collective-permute-done = bf16[8,128,256]{2,1,0:T(8,128)(2,1)S(1)} collective-permute-done((bf16[8,128,256]{2,1,0:T(8,128)(2,1)S(1)}, bf16[8,128,256]{2,1,0:T(8,128)(2,1)S(1)}, u32[]{:S(2)}, u32[]{:S(2)}) %collective-permute-start) | collective-permute-done | bytes 524320 | tf_op jit(solution)/shard_map/while/body/eval_jaxpr/ppermute | solution.py:10
  141.3 9.6 collective-permute-done
  203.1 9.6 collective-permute-done
  264.8 9.6 collective-permute-done
  365.1 15.8 %fusion.65 = f32[8,128,256]{2,0,1:T(8,128)S(1)} fusion(f32[8,128,256]{2,0,1:T(8,128)} %get-tuple-element.494, f32[8,4,128,256]{3,1,2,0:T(4,128)} %all-to-all-done, f32[8,4,8]{2,1,0:T(4,128)S(1)} %fusion.89), kind=kOutput, calls=%fused_computation.79 | convolution fusion | flops 100925440 | bytes 6292480 | tf_op jit(solution)/shard_map/scr,scif->rif/dot_general | solution.py:108
  389.4 21.2 %copy.51 = bf16[1,1,16,32,128,128]{4,5,3,2,1,0:T(8,128)(2,1)} copy(bf16[1,1,16,32,128,128]{5,4,3,2,1,0:T(8,128)(2,1)} %bitcast.174) | data formatting | bytes 33554432 | tf_op args[4]
  425.9 365.8 %while.35 = (s32[]{:T(128)}, f32[8,128,256]{2,0,1:T(8,128)}, s32[]{:T(128)}, s32[16,32]{1,0:T(8,128)}, s32[16]{0:T(128)S(1)}, /*index=5*/bf16[16,32,128,128]{2,3...) while((s32[]{:T(128)}, f32[8,128,256]{2,0,1:T(8,128)}, ...), condition=%wide.region_4.6_spmd.clone, body=%wide.region_3.5_spmd.clone.sunk | while | flops 370411264 | bytes 22025748 | solution.py:122
  452.3 11.6 %collective-permute-done.1 = f32[8,128,256]{2,0,1:T(8,128)} collective-permute-done((f32[8,128,256]{2,0,1:T(8,128)}, f32[8,128,256]{2,0,1:T(8,128)}, u32[]{:S(2)}, u32[]{:S(2)}) %collective-permute-start.1) | collective-permute-done | bytes 1048608 | tf_op jit(solution)/shard_map/while/body/eval_jaxpr/ppermute | solution.py:10
  475.8 12.8 %collective-permute-done.1 = f32[8,128,256]{2,0,1:T(8,128)} collective-permute-done((f32[8,128,256]{2,0,1:T(8,128)}, f32[8,128,256]{2,0,1:T(8,128)}, u32[]{:S(2)}, u32[]{:S(2)}) %collective-permute-start.1) | collective-permute-done | bytes 1048608 | tf_op jit(solution)/shard_map/while/body/eval_jaxpr/ppermute | solution.py:10
  500.5 12.8 %collective-permute-done.1 = f32[8,128,256]{2,0,1:T(8,128)} collective-permute-done((f32[8,128,256]{2,0,1:T(8,128)}, f32[8,128,256]{2,0,1:T(8,128)}, u32[]{:S(2)}, u32[]{:S(2)}) %collective-permute-start.1) | collective-permute-done | bytes 1048608 | tf_op jit(solution)/shard_map/while/body/eval_jaxpr/ppermute | solution.py:10
  525.2 12.8 %collective-permute-done.1 = f32[8,128,256]{2,0,1:T(8,128)} collective-permute-done((f32[8,128,256]{2,0,1:T(8,128)}, f32[8,128,256]{2,0,1:T(8,128)}, u32[]{:S(2)}, u32[]{:S(2)}) %collective-permute-start.1) | collective-permute-done | bytes 1048608 | tf_op jit(solution)/shard_map/while/body/eval_jaxpr/ppermute | solution.py:10
  550.0 12.8 %collective-permute-done.1 = f32[8,128,256]{2,0,1:T(8,128)} collective-permute-done((f32[8,128,256]{2,0,1:T(8,128)}, f32[8,128,256]{2,0,1:T(8,128)}, u32[]{:S(2)}, u32[]{:S(2)}) %collective-permute-start.1) | collective-permute-done | bytes 1048608 | tf_op jit(solution)/shard_map/while/body/eval_jaxpr/ppermute | solution.py:10
  574.7 12.8 %collective-permute-done.1 = f32[8,128,256]{2,0,1:T(8,128)} collective-permute-done((f32[8,128,256]{2,0,1:T(8,128)}, f32[8,128,256]{2,0,1:T(8,128)}, u32[]{:S(2)}, u32[]{:S(2)}) %collective-permute-start.1) | collective-permute-done | bytes 1048608 | tf_op jit(solution)/shard_map/while/body/eval_jaxpr/ppermute | solution.py:10
  599.4 12.8 %collective-permute-done.1 = f32[8,128,256]{2,0,1:T(8,128)} collective-permute-done((f32[8,128,256]{2,0,1:T(8,128)}, f32[8,128,256]{2,0,1:T(8,128)}, u32[]{:S(2)}, u32[]{:S(2)}) %collective-permute-start.1) | collective-permute-done | bytes 1048608 | tf_op jit(solution)/shard_map/while/body/eval_jaxpr/ppermute | solution.py:10
  624.1 12.8 %collective-permute-done.1 = f32[8,128,256]{2,0,1:T(8,128)} collective-permute-done((f32[8,128,256]{2,0,1:T(8,128)}, f32[8,128,256]{2,0,1:T(8,128)}, u32[]{:S(2)}, u32[]{:S(2)}) %collective-permute-start.1) | collective-permute-done | bytes 1048608 | tf_op jit(solution)/shard_map/while/body/eval_jaxpr/ppermute | solution.py:10
  648.8 12.8 %collective-permute-done.1 = f32[8,128,256]{2,0,1:T(8,128)} collective-permute-done((f32[8,128,256]{2,0,1:T(8,128)}, f32[8,128,256]{2,0,1:T(8,128)}, u32[]{:S(2)}, u32[]{:S(2)}) %collective-permute-start.1) | collective-permute-done | bytes 1048608 | tf_op jit(solution)/shard_map/while/body/eval_jaxpr/ppermute | solution.py:10
  673.5 12.8 %collective-permute-done.1 = f32[8,128,256]{2,0,1:T(8,128)} collective-permute-done((f32[8,128,256]{2,0,1:T(8,128)}, f32[8,128,256]{2,0,1:T(8,128)}, u32[]{:S(2)}, u32[]{:S(2)}) %collective-permute-start.1) | collective-permute-done | bytes 1048608 | tf_op jit(solution)/shard_map/while/body/eval_jaxpr/ppermute | solution.py:10
  698.2 12.8 %collective-permute-done.1 = f32[8,128,256]{2,0,1:T(8,128)} collective-permute-done((f32[8,128,256]{2,0,1:T(8,128)}, f32[8,128,256]{2,0,1:T(8,128)}, u32[]{:S(2)}, u32[]{:S(2)}) %collective-permute-start.1) | collective-permute-done | bytes 1048608 | tf_op jit(solution)/shard_map/while/body/eval_jaxpr/ppermute | solution.py:10
  722.9 12.8 %collective-permute-done.1 = f32[8,128,256]{2,0,1:T(8,128)} collective-permute-done((f32[8,128,256]{2,0,1:T(8,128)}, f32[8,128,256]{2,0,1:T(8,128)}, u32[]{:S(2)}, u32[]{:S(2)}) %collective-permute-start.1) | collective-permute-done | bytes 1048608 | tf_op jit(solution)/shard_map/while/body/eval_jaxpr/ppermute | solution.py:10
  747.6 12.8 %collective-permute-done.1 = f32[8,128,256]{2,0,1:T(8,128)} collective-permute-done((f32[8,128,256]{2,0,1:T(8,128)}, f32[8,128,256]{2,0,1:T(8,128)}, u32[]{:S(2)}, u32[]{:S(2)}) %collective-permute-start.1) | collective-permute-done | bytes 1048608 | tf_op jit(solution)/shard_map/while/body/eval_jaxpr/ppermute | solution.py:10
  772.3 12.8 %collective-permute-done.1 = f32[8,128,256]{2,0,1:T(8,128)} collective-permute-done((f32[8,128,256]{2,0,1:T(8,128)}, f32[8,128,256]{2,0,1:T(8,128)}, u32[]{:S(2)}, u32[]{:S(2)}) %collective-permute-start.1) | collective-permute-done | bytes 1048608 | tf_op jit(solution)/shard_map/while/body/eval_jaxpr/ppermute | solution.py:10
  796.8 153.1 %all-reduce.2.cloned.1.call-done = f32[256,256]{0,1:T(8,128)} async-done(((f32[256,256]{0,1:T(8,128)}), f32[256,256]{0,1:T(8,128)}) %all-reduce.2.cloned.1.call-update) | async-done | bytes 262160 | tf_op jit(solution)/shard_map/psum | solution.py:145
  (424 shorter events, 520.3 us)
Async XLA Ops:
  31.5 333.6 %all-to-all-start = ((f32[8,4,128,256]{3,1,2,0:T(4,128)}), f32[8,4,128,256]{3,1,2,0:T(4,128)}, u32[]{:S(2)}, u32[]{:S(2)}) async-start(f32[8,4,128,256]{3,1,2,0:T(4,128)} %copy.55), calls=%async_computation | async-start | bytes 8388608 | tf_op jit(solution)/shard_map/all_to_all | solution.py:101
  68.0 16.4 %collective-permute-start = (bf16[8,128,256]{2,1,0:T(8,128)(2,1)S(1)}, bf16[8,128,256]{2,1,0:T(8,128)(2,1)S(1)}, u32[]{:S(2)}, u32[]{:S(2)}) collective-permute-start(bf16[8,128,256]{2,1,0:T(8,128)(2,1)S(1)} %get-tuple-element.727), channel_id=1, source_target_pairs={{0,1},{1,2},{2,3},{3,4},{4,5},{5,6},{6,7},{7,8},{8,9},{9,10},{10,1... | collective-permute-start | bytes 1572872 | tf_op jit(solution)/shard_map/while/body/eval_jaxpr/ppermute | solution.py:10
  92.8 16.9 %collective-permute-start = (bf16[8,128,256]{2,1,0:T(8,128)(2,1)S(1)}, bf16[8,128,256]{2,1,0:T(8,128)(2,1)S(1)}, u32[]{:S(2)}, u32[]{:S(2)}) collective-permute-start(bf16[8,128,256]{2,1,0:T(8,128)(2,1)S(1)} %get-tuple-element.727), channel_id=1, source_target_pairs={{0,1},{1,2},{2,3},{3,4},{4,5},{5,6},{6,7},{7,8},{8,9},{9,10},{10,1... | collective-permute-start | bytes 1572872 | tf_op jit(solution)/shard_map/while/body/eval_jaxpr/ppermute | solution.py:10
  138.7 12.2 %collective-permute-start = (bf16[8,128,256]{2,1,0:T(8,128)(2,1)S(1)}, bf16[8,128,256]{2,1,0:T(8,128)(2,1)S(1)}, u32[]{:S(2)}, u32[]{:S(2)}) collective-permute-start(bf16[8,128,256]{2,1,0:T(8,128)(2,1)S(1)} %get-tuple-element.727), channel_id=1, source_target_pairs={{0,1},{1,2},{2,3},{3,4},{4,5},{5,6},{6,7},{7,8},{8,9},{9,10},{10,1... | collective-permute-start | bytes 1572872 | tf_op jit(solution)/shard_map/while/body/eval_jaxpr/ppermute | solution.py:10
  200.4 12.2 %collective-permute-start = (bf16[8,128,256]{2,1,0:T(8,128)(2,1)S(1)}, bf16[8,128,256]{2,1,0:T(8,128)(2,1)S(1)}, u32[]{:S(2)}, u32[]{:S(2)}) collective-permute-start(bf16[8,128,256]{2,1,0:T(8,128)(2,1)S(1)} %get-tuple-element.727), channel_id=1, source_target_pairs={{0,1},{1,2},{2,3},{3,4},{4,5},{5,6},{6,7},{7,8},{8,9},{9,10},{10,1... | collective-permute-start | bytes 1572872 | tf_op jit(solution)/shard_map/while/body/eval_jaxpr/ppermute | solution.py:10
  262.2 12.2 %collective-permute-start = (bf16[8,128,256]{2,1,0:T(8,128)(2,1)S(1)}, bf16[8,128,256]{2,1,0:T(8,128)(2,1)S(1)}, u32[]{:S(2)}, u32[]{:S(2)}) collective-permute-start(bf16[8,128,256]{2,1,0:T(8,128)(2,1)S(1)} %get-tuple-element.727), channel_id=1, source_target_pairs={{0,1},{1,2},{2,3},{3,4},{4,5},{5,6},{6,7},{7,8},{8,9},{9,10},{10,1... | collective-permute-start | bytes 1572872 | tf_op jit(solution)/shard_map/while/body/eval_jaxpr/ppermute | solution.py:10
  324.0 12.2 %collective-permute-start = (bf16[8,128,256]{2,1,0:T(8,128)(2,1)S(1)}, bf16[8,128,256]{2,1,0:T(8,128)(2,1)S(1)}, u32[]{:S(2)}, u32[]{:S(2)}) collective-permute-start(bf16[8,128,256]{2,1,0:T(8,128)(2,1)S(1)} %get-tuple-element.727), channel_id=1, source_target_pairs={{0,1},{1,2},{2,3},{3,4},{4,5},{5,6},{6,7},{7,8},{8,9},{9,10},{10,1... | collective-permute-start | bytes 1572872 | tf_op jit(solution)/shard_map/while/body/eval_jaxpr/ppermute | solution.py:10
  385.7 36.3 %all-to-all-start.1 = ((bf16[8,4,128,256]{3,2,1,0:T(8,128)(2,1)}), bf16[8,4,128,256]{3,2,1,0:T(8,128)(2,1)S(1)}, u32[]{:S(2)}, u32[]{:S(2)}) async-start(bf16[8,4,128,256]{3,2,1,0:T(8,128)(2,1)} %copy.62), calls=%async_computation.1 | async-start | bytes 4194304 | tf_op jit(solution)/shard_map/all_to_all | solution.py:129
  389.3 560.6 %all-reduce.2.cloned.1.call-start = ((), (), s32[]{:S(2)}) async-start(), calls=%async_computation.2 | async-start | bytes 524288 | tf_op jit(solution)/shard_map/psum | solution.py:145
  425.9 13.3 %collective-permute-start.1 = (f32[8,128,256]{2,0,1:T(8,128)}, f32[8,128,256]{2,0,1:T(8,128)}, u32[]{:S(2)}, u32[]{:S(2)}) collective-permute-start(f32[8,128,256]{2,0,1:T(8,128)} %get-tuple-element.763), channel_id=1, source_target_pairs={{0,1},{1,2},{2,3},{3,4},{4,5},{5,6},{6,7},{7,8},{8,9},{9,10},{10,1... | collective-permute-start | bytes 3145736 | tf_op jit(solution)/shard_map/while/body/eval_jaxpr/ppermute | solution.py:10
  445.8 18.2 %collective-permute-start.1 = (f32[8,128,256]{2,0,1:T(8,128)}, f32[8,128,256]{2,0,1:T(8,128)}, u32[]{:S(2)}, u32[]{:S(2)}) collective-permute-start(f32[8,128,256]{2,0,1:T(8,128)} %get-tuple-element.763), channel_id=1, source_target_pairs={{0,1},{1,2},{2,3},{3,4},{4,5},{5,6},{6,7},{7,8},{8,9},{9,10},{10,1... | collective-permute-start | bytes 3145736 | tf_op jit(solution)/shard_map/while/body/eval_jaxpr/ppermute | solution.py:10
  470.5 18.2 %collective-permute-start.1 = (f32[8,128,256]{2,0,1:T(8,128)}, f32[8,128,256]{2,0,1:T(8,128)}, u32[]{:S(2)}, u32[]{:S(2)}) collective-permute-start(f32[8,128,256]{2,0,1:T(8,128)} %get-tuple-element.763), channel_id=1, source_target_pairs={{0,1},{1,2},{2,3},{3,4},{4,5},{5,6},{6,7},{7,8},{8,9},{9,10},{10,1... | collective-permute-start | bytes 3145736 | tf_op jit(solution)/shard_map/while/body/eval_jaxpr/ppermute | solution.py:10
  495.2 18.2 %collective-permute-start.1 = (f32[8,128,256]{2,0,1:T(8,128)}, f32[8,128,256]{2,0,1:T(8,128)}, u32[]{:S(2)}, u32[]{:S(2)}) collective-permute-start(f32[8,128,256]{2,0,1:T(8,128)} %get-tuple-element.763), channel_id=1, source_target_pairs={{0,1},{1,2},{2,3},{3,4},{4,5},{5,6},{6,7},{7,8},{8,9},{9,10},{10,1... | collective-permute-start | bytes 3145736 | tf_op jit(solution)/shard_map/while/body/eval_jaxpr/ppermute | solution.py:10
  519.9 18.2 %collective-permute-start.1 = (f32[8,128,256]{2,0,1:T(8,128)}, f32[8,128,256]{2,0,1:T(8,128)}, u32[]{:S(2)}, u32[]{:S(2)}) collective-permute-start(f32[8,128,256]{2,0,1:T(8,128)} %get-tuple-element.763), channel_id=1, source_target_pairs={{0,1},{1,2},{2,3},{3,4},{4,5},{5,6},{6,7},{7,8},{8,9},{9,10},{10,1... | collective-permute-start | bytes 3145736 | tf_op jit(solution)/shard_map/while/body/eval_jaxpr/ppermute | solution.py:10
  544.6 18.2 %collective-permute-start.1 = (f32[8,128,256]{2,0,1:T(8,128)}, f32[8,128,256]{2,0,1:T(8,128)}, u32[]{:S(2)}, u32[]{:S(2)}) collective-permute-start(f32[8,128,256]{2,0,1:T(8,128)} %get-tuple-element.763), channel_id=1, source_target_pairs={{0,1},{1,2},{2,3},{3,4},{4,5},{5,6},{6,7},{7,8},{8,9},{9,10},{10,1... | collective-permute-start | bytes 3145736 | tf_op jit(solution)/shard_map/while/body/eval_jaxpr/ppermute | solution.py:10
  569.3 18.2 %collective-permute-start.1 = (f32[8,128,256]{2,0,1:T(8,128)}, f32[8,128,256]{2,0,1:T(8,128)}, u32[]{:S(2)}, u32[]{:S(2)}) collective-permute-start(f32[8,128,256]{2,0,1:T(8,128)} %get-tuple-element.763), channel_id=1, source_target_pairs={{0,1},{1,2},{2,3},{3,4},{4,5},{5,6},{6,7},{7,8},{8,9},{9,10},{10,1... | collective-permute-start | bytes 3145736 | tf_op jit(solution)/shard_map/while/body/eval_jaxpr/ppermute | solution.py:10
  594.0 18.2 %collective-permute-start.1 = (f32[8,128,256]{2,0,1:T(8,128)}, f32[8,128,256]{2,0,1:T(8,128)}, u32[]{:S(2)}, u32[]{:S(2)}) collective-permute-start(f32[8,128,256]{2,0,1:T(8,128)} %get-tuple-element.763), channel_id=1, source_target_pairs={{0,1},{1,2},{2,3},{3,4},{4,5},{5,6},{6,7},{7,8},{8,9},{9,10},{10,1... | collective-permute-start | bytes 3145736 | tf_op jit(solution)/shard_map/while/body/eval_jaxpr/ppermute | solution.py:10
  618.7 18.2 %collective-permute-start.1 = (f32[8,128,256]{2,0,1:T(8,128)}, f32[8,128,256]{2,0,1:T(8,128)}, u32[]{:S(2)}, u32[]{:S(2)}) collective-permute-start(f32[8,128,256]{2,0,1:T(8,128)} %get-tuple-element.763), channel_id=1, source_target_pairs={{0,1},{1,2},{2,3},{3,4},{4,5},{5,6},{6,7},{7,8},{8,9},{9,10},{10,1... | collective-permute-start | bytes 3145736 | tf_op jit(solution)/shard_map/while/body/eval_jaxpr/ppermute | solution.py:10
  643.5 18.2 %collective-permute-start.1 = (f32[8,128,256]{2,0,1:T(8,128)}, f32[8,128,256]{2,0,1:T(8,128)}, u32[]{:S(2)}, u32[]{:S(2)}) collective-permute-start(f32[8,128,256]{2,0,1:T(8,128)} %get-tuple-element.763), channel_id=1, source_target_pairs={{0,1},{1,2},{2,3},{3,4},{4,5},{5,6},{6,7},{7,8},{8,9},{9,10},{10,1... | collective-permute-start | bytes 3145736 | tf_op jit(solution)/shard_map/while/body/eval_jaxpr/ppermute | solution.py:10
  668.2 18.2 %collective-permute-start.1 = (f32[8,128,256]{2,0,1:T(8,128)}, f32[8,128,256]{2,0,1:T(8,128)}, u32[]{:S(2)}, u32[]{:S(2)}) collective-permute-start(f32[8,128,256]{2,0,1:T(8,128)} %get-tuple-element.763), channel_id=1, source_target_pairs={{0,1},{1,2},{2,3},{3,4},{4,5},{5,6},{6,7},{7,8},{8,9},{9,10},{10,1... | collective-permute-start | bytes 3145736 | tf_op jit(solution)/shard_map/while/body/eval_jaxpr/ppermute | solution.py:10
  692.9 18.2 %collective-permute-start.1 = (f32[8,128,256]{2,0,1:T(8,128)}, f32[8,128,256]{2,0,1:T(8,128)}, u32[]{:S(2)}, u32[]{:S(2)}) collective-permute-start(f32[8,128,256]{2,0,1:T(8,128)} %get-tuple-element.763), channel_id=1, source_target_pairs={{0,1},{1,2},{2,3},{3,4},{4,5},{5,6},{6,7},{7,8},{8,9},{9,10},{10,1... | collective-permute-start | bytes 3145736 | tf_op jit(solution)/shard_map/while/body/eval_jaxpr/ppermute | solution.py:10
  717.6 18.2 %collective-permute-start.1 = (f32[8,128,256]{2,0,1:T(8,128)}, f32[8,128,256]{2,0,1:T(8,128)}, u32[]{:S(2)}, u32[]{:S(2)}) collective-permute-start(f32[8,128,256]{2,0,1:T(8,128)} %get-tuple-element.763), channel_id=1, source_target_pairs={{0,1},{1,2},{2,3},{3,4},{4,5},{5,6},{6,7},{7,8},{8,9},{9,10},{10,1... | collective-permute-start | bytes 3145736 | tf_op jit(solution)/shard_map/while/body/eval_jaxpr/ppermute | solution.py:10
  742.3 18.2 %collective-permute-start.1 = (f32[8,128,256]{2,0,1:T(8,128)}, f32[8,128,256]{2,0,1:T(8,128)}, u32[]{:S(2)}, u32[]{:S(2)}) collective-permute-start(f32[8,128,256]{2,0,1:T(8,128)} %get-tuple-element.763), channel_id=1, source_target_pairs={{0,1},{1,2},{2,3},{3,4},{4,5},{5,6},{6,7},{7,8},{8,9},{9,10},{10,1... | collective-permute-start | bytes 3145736 | tf_op jit(solution)/shard_map/while/body/eval_jaxpr/ppermute | solution.py:10
  767.0 18.2 %collective-permute-start.1 = (f32[8,128,256]{2,0,1:T(8,128)}, f32[8,128,256]{2,0,1:T(8,128)}, u32[]{:S(2)}, u32[]{:S(2)}) collective-permute-start(f32[8,128,256]{2,0,1:T(8,128)} %get-tuple-element.763), channel_id=1, source_target_pairs={{0,1},{1,2},{2,3},{3,4},{4,5},{5,6},{6,7},{7,8},{8,9},{9,10},{10,1... | collective-permute-start | bytes 3145736 | tf_op jit(solution)/shard_map/while/body/eval_jaxpr/ppermute | solution.py:10
  (48 other events, 540.2 us)
Sparse Core Ops, SparseCore 0:
  795.8 154.0 all-reduce.1
where the time goes:
time: 967 us; the launch traced here: 959 us
  waiting for transfers between devices  483 us (50%)
  matrix products  275 us (28%)
  local copies, waits for them, and re-layouts  122 us (13%)
  other arithmetic  46.4 us (5%)
  starting transfers between devices  16.2 us (2%)
  between operations  14.5 us (1%)
    ppermute x30, waiting for transfers between devices, shifted(): lax.ppermute(value, axis, [(i, (i + by) % size) for i in range(size)])  330 us
    psum x1, waiting for transfers between devices, local(): grad_weight = lax.psum(weight_term, ('grp', 'blk')) * grad_scale  153 us
    dot_general x16, matrix products, backward_block(): return jnp.einsum('tr,tjf->rjf', placing, product, precision=highest)  104 us
    dot_general x16, matrix products, forward_block(): return jnp.einsum('tr,tif->rif', placing, product, precision=highest)  72.6 us
    dot_general x16, matrix products, forward_block(): jnp.einsum('tij,tjf->tif', blk_vals, picked, preferred_element_type=jnp.f...  34.1 us
    dot_general x16, matrix products, backward_block(): jnp.einsum('tij,tif->tjf', blk_vals, picked, preferred_element_type=jnp.f...  32.7 us
    unnamed x20, local copies, waits for them, and re-layouts  22.8 us
    convert_element_type x32, other arithmetic, block_parts(): live_mask = (slot_range < blk_count).astype(jnp.float32)  20.7 us
  transfers between devices with their start and end apart: 33, of which 31 were waited for; matrix products, arithmetic and copies ran while one was open for 29% of the time, Pallas kernels for 0%

commit v1 on v0

--- a/solution.py
+++ b/solution.py
@@ -142,7 +142,7 @@
         feats, grad_rows, (((0,), (0,)), ((), ())), preferred_element_type=jnp.float32
     )
     grad_scale = 1.0 / math.sqrt(rows_dev * n_blocks * n_groups)
-    grad_weight = lax.psum(weight_term, ("grp", "blk")) * grad_scale
+    grad_weight = jnp.sum(lax.all_gather(weight_term, ("grp", "blk")), axis=0) * grad_scale
     grad_feats = lax.dot_general(
         grad_rows, weight, (((1,), (1,)), ((), ())), preferred_element_type=jnp.float32
     ).astype(jnp.bfloat16)

time: 967 us -> 1080 us (1.12)
  waiting for transfers between devices: 483 us -> 579 us
  local copies, waits for them, and re-layouts: 122 us -> 141 us
    all_gather x0 -> x1, waiting for transfers between devices: none -> 249 us  [local(): lax.all_gather(weight_term, ('grp', 'blk'))]
    psum x1 -> x0, waiting for transfers between devices: 153 us -> none  [local(): grad_weight = lax.psum(weight_term, ('grp', 'blk')) * grad_scale]
    unnamed x20 -> x23, local copies, waits for them, and re-layouts: 22.8 us -> 42.5 us
  transfers between devices with their start and end apart: 33 -> 33, of which waited for: 31 -> 31; matrix products, arithmetic and copies ran while one was open for 29% -> 26% of each run, Pallas kernels for 0% -> 0%
where the time goes in v1:
time: 1080 us; the launch traced here: 1070 us
  waiting for transfers between devices  579 us (54%)
  matrix products  267 us (25%)
  local copies, waits for them, and re-layouts  141 us (13%)
  other arithmetic  49.6 us (5%)
  starting transfers between devices  16.5 us (2%)
  between operations  14.5 us (1%)
    ppermute x30, waiting for transfers between devices, shifted(): lax.ppermute(value, axis, [(i, (i + by) % size) for i in range(size)])  330 us
    all_gather x1, waiting for transfers between devices, local(): lax.all_gather(weight_term, ('grp', 'blk'))  249 us
    dot_general x16, matrix products, backward_block(): return jnp.einsum('tr,tjf->rjf', placing, product, precision=highest)  104 us
    dot_general x16, matrix products, forward_block(): return jnp.einsum('tr,tif->rif', placing, product, precision=highest)  72.6 us
    unnamed x23, local copies, waits for them, and re-layouts  42.5 us
    dot_general x16, matrix products, forward_block(): jnp.einsum('tij,tjf->tif', blk_vals, picked, preferred_element_type=jnp.f...  34.1 us
    dot_general x16, matrix products, backward_block(): jnp.einsum('tij,tif->tjf', blk_vals, picked, preferred_element_type=jnp.f...  32.7 us
  transfers between devices with their start and end apart: 33, of which 31 were waited for; matrix products, arithmetic and copies ran while one was open for 26% of the time, Pallas kernels for 0%

profile of v1, /device:TPU:1, one launch (start us, length us, event | category | flops | bytes accessed | tf_op | source)
XLA Modules:
  0.0 1069.1 jit_solution(10728234638235846559)
XLA Ops:
  51.5 313.7 %while.34 = (s32[]{:T(128)}, bf16[8,128,256]{2,1,0:T(8,128)(2,1)S(1)}, f32[8,128,256]{2,0,1:T(8,128)}, s32[]{:T(128)}, s32[16,32]{1,0:T(8,128)}, /*index=5*/s32[...) while((s32[]{:T(128)}, ...), condition=%wide.region_1.3_spmd.clone, body=%wide.region_0.2_spmd.clone.sunk | while | flops 370411264 | bytes 29365836 | solution.py:82
  73.2 11.3 %collective-permute-done = bf16[8,128,256]{2,1,0:T(8,128)(2,1)S(1)} collective-permute-done((bf16[8,128,256]{2,1,0:T(8,128)(2,1)S(1)}, bf16[8,128,256]{2,1,0:T(8,128)(2,1)S(1)}, u32[]{:S(2)}, u32[]{:S(2)}) %collective-permute-start) | collective-permute-done | bytes 524320 | tf_op jit(solution)/shard_map/while/body/eval_jaxpr/ppermute | solution.py:10
  95.5 14.4 %collective-permute-done = bf16[8,128,256]{2,1,0:T(8,128)(2,1)S(1)} collective-permute-done((bf16[8,128,256]{2,1,0:T(8,128)(2,1)S(1)}, bf16[8,128,256]{2,1,0:T(8,128)(2,1)S(1)}, u32[]{:S(2)}, u32[]{:S(2)}) %collective-permute-start) | collective-permute-done | bytes 524320 | tf_op jit(solution)/shard_map/while/body/eval_jaxpr/ppermute | solution.py:10
  162.1 9.6 collective-permute-done
  182.6 9.6 collective-permute-done
  264.9 9.6 collective-permute-done
  380.8 21.3 %copy.49 = bf16[1,1,16,32,128,128]{4,5,3,2,1,0:T(8,128)(2,1)} copy(bf16[1,1,16,32,128,128]{5,4,3,2,1,0:T(8,128)(2,1)} %bitcast.179) | data formatting | bytes 33554432 | tf_op args[4]
  417.4 366.3 %while.35 = (s32[]{:T(128)}, f32[8,128,256]{2,0,1:T(8,128)}, s32[]{:T(128)}, s32[16,32]{1,0:T(8,128)}, s32[16]{0:T(128)S(1)}, /*index=5*/bf16[16,32,128,128]{2,3...) while((s32[]{:T(128)}, f32[8,128,256]{2,0,1:T(8,128)}, ...), condition=%wide.region_4.6_spmd.clone, body=%wide.region_3.5_spmd.clone.sunk | while | flops 370411264 | bytes 22025748 | solution.py:122
  444.1 11.6 %collective-permute-done.1 = f32[8,128,256]{2,0,1:T(8,128)} collective-permute-done((f32[8,128,256]{2,0,1:T(8,128)}, f32[8,128,256]{2,0,1:T(8,128)}, u32[]{:S(2)}, u32[]{:S(2)}) %collective-permute-start.1) | collective-permute-done | bytes 1048608 | tf_op jit(solution)/shard_map/while/body/eval_jaxpr/ppermute | solution.py:10
  467.6 12.8 %collective-permute-done.1 = f32[8,128,256]{2,0,1:T(8,128)} collective-permute-done((f32[8,128,256]{2,0,1:T(8,128)}, f32[8,128,256]{2,0,1:T(8,128)}, u32[]{:S(2)}, u32[]{:S(2)}) %collective-permute-start.1) | collective-permute-done | bytes 1048608 | tf_op jit(solution)/shard_map/while/body/eval_jaxpr/ppermute | solution.py:10
  492.4 12.8 %collective-permute-done.1 = f32[8,128,256]{2,0,1:T(8,128)} collective-permute-done((f32[8,128,256]{2,0,1:T(8,128)}, f32[8,128,256]{2,0,1:T(8,128)}, u32[]{:S(2)}, u32[]{:S(2)}) %collective-permute-start.1) | collective-permute-done | bytes 1048608 | tf_op jit(solution)/shard_map/while/body/eval_jaxpr/ppermute | solution.py:10
  517.1 12.8 %collective-permute-done.1 = f32[8,128,256]{2,0,1:T(8,128)} collective-permute-done((f32[8,128,256]{2,0,1:T(8,128)}, f32[8,128,256]{2,0,1:T(8,128)}, u32[]{:S(2)}, u32[]{:S(2)}) %collective-permute-start.1) | collective-permute-done | bytes 1048608 | tf_op jit(solution)/shard_map/while/body/eval_jaxpr/ppermute | solution.py:10
  541.8 12.8 %collective-permute-done.1 = f32[8,128,256]{2,0,1:T(8,128)} collective-permute-done((f32[8,128,256]{2,0,1:T(8,128)}, f32[8,128,256]{2,0,1:T(8,128)}, u32[]{:S(2)}, u32[]{:S(2)}) %collective-permute-start.1) | collective-permute-done | bytes 1048608 | tf_op jit(solution)/shard_map/while/body/eval_jaxpr/ppermute | solution.py:10
  566.5 12.8 %collective-permute-done.1 = f32[8,128,256]{2,0,1:T(8,128)} collective-permute-done((f32[8,128,256]{2,0,1:T(8,128)}, f32[8,128,256]{2,0,1:T(8,128)}, u32[]{:S(2)}, u32[]{:S(2)}) %collective-permute-start.1) | collective-permute-done | bytes 1048608 | tf_op jit(solution)/shard_map/while/body/eval_jaxpr/ppermute | solution.py:10
  591.2 12.8 %collective-permute-done.1 = f32[8,128,256]{2,0,1:T(8,128)} collective-permute-done((f32[8,128,256]{2,0,1:T(8,128)}, f32[8,128,256]{2,0,1:T(8,128)}, u32[]{:S(2)}, u32[]{:S(2)}) %collective-permute-start.1) | collective-permute-done | bytes 1048608 | tf_op jit(solution)/shard_map/while/body/eval_jaxpr/ppermute | solution.py:10
  616.0 12.8 %collective-permute-done.1 = f32[8,128,256]{2,0,1:T(8,128)} collective-permute-done((f32[8,128,256]{2,0,1:T(8,128)}, f32[8,128,256]{2,0,1:T(8,128)}, u32[]{:S(2)}, u32[]{:S(2)}) %collective-permute-start.1) | collective-permute-done | bytes 1048608 | tf_op jit(solution)/shard_map/while/body/eval_jaxpr/ppermute | solution.py:10
  640.7 12.8 %collective-permute-done.1 = f32[8,128,256]{2,0,1:T(8,128)} collective-permute-done((f32[8,128,256]{2,0,1:T(8,128)}, f32[8,128,256]{2,0,1:T(8,128)}, u32[]{:S(2)}, u32[]{:S(2)}) %collective-permute-start.1) | collective-permute-done | bytes 1048608 | tf_op jit(solution)/shard_map/while/body/eval_jaxpr/ppermute | solution.py:10
  665.4 12.8 %collective-permute-done.1 = f32[8,128,256]{2,0,1:T(8,128)} collective-permute-done((f32[8,128,256]{2,0,1:T(8,128)}, f32[8,128,256]{2,0,1:T(8,128)}, u32[]{:S(2)}, u32[]{:S(2)}) %collective-permute-start.1) | collective-permute-done | bytes 1048608 | tf_op jit(solution)/shard_map/while/body/eval_jaxpr/ppermute | solution.py:10
  690.1 12.8 %collective-permute-done.1 = f32[8,128,256]{2,0,1:T(8,128)} collective-permute-done((f32[8,128,256]{2,0,1:T(8,128)}, f32[8,128,256]{2,0,1:T(8,128)}, u32[]{:S(2)}, u32[]{:S(2)}) %collective-permute-start.1) | collective-permute-done | bytes 1048608 | tf_op jit(solution)/shard_map/while/body/eval_jaxpr/ppermute | solution.py:10
  714.9 12.8 %collective-permute-done.1 = f32[8,128,256]{2,0,1:T(8,128)} collective-permute-done((f32[8,128,256]{2,0,1:T(8,128)}, f32[8,128,256]{2,0,1:T(8,128)}, u32[]{:S(2)}, u32[]{:S(2)}) %collective-permute-start.1) | collective-permute-done | bytes 1048608 | tf_op jit(solution)/shard_map/while/body/eval_jaxpr/ppermute | solution.py:10
  739.6 12.8 %collective-permute-done.1 = f32[8,128,256]{2,0,1:T(8,128)} collective-permute-done((f32[8,128,256]{2,0,1:T(8,128)}, f32[8,128,256]{2,0,1:T(8,128)}, u32[]{:S(2)}, u32[]{:S(2)}) %collective-permute-start.1) | collective-permute-done | bytes 1048608 | tf_op jit(solution)/shard_map/while/body/eval_jaxpr/ppermute | solution.py:10
  764.3 12.8 %collective-permute-done.1 = f32[8,128,256]{2,0,1:T(8,128)} collective-permute-done((f32[8,128,256]{2,0,1:T(8,128)}, f32[8,128,256]{2,0,1:T(8,128)}, u32[]{:S(2)}, u32[]{:S(2)}) %collective-permute-start.1) | collective-permute-done | bytes 1048608 | tf_op jit(solution)/shard_map/while/body/eval_jaxpr/ppermute | solution.py:10
  788.8 248.6 %all-gather.3.cloned.1.call-done = f32[32768,256]{0,1:T(8,128)} async-done(((f32[256,256]{0,1:T(8,128)}), f32[32768,256]{0,1:T(8,128)}) %all-gather.3.cloned.1.call-update) | async-done | bytes 33554448 | tf_op jit(solution)/shard_map/all_gather | solution.py:145
  1037.4 19.6 %copy.72 = f32[32,8,128,256]{3,2,1,0:T(8,128)S(1)} copy(f32[32,8,128,256]{3,1,2,0:T(8,128)} %bitcast.181) | data formatting | bytes 67108864
  (428 shorter events, 530.8 us)
Async XLA Ops:
  31.5 333.7 %all-to-all-start = ((f32[8,4,128,256]{3,1,2,0:T(4,128)}), f32[8,4,128,256]{3,1,2,0:T(4,128)}, u32[]{:S(2)}, u32[]{:S(2)}) async-start(f32[8,4,128,256]{3,1,2,0:T(4,128)} %copy.53), calls=%async_computation | async-start | bytes 8388608 | tf_op jit(solution)/shard_map/all_to_all | solution.py:101
  68.1 16.4 %collective-permute-start = (bf16[8,128,256]{2,1,0:T(8,128)(2,1)S(1)}, bf16[8,128,256]{2,1,0:T(8,128)(2,1)S(1)}, u32[]{:S(2)}, u32[]{:S(2)}) collective-permute-start(bf16[8,128,256]{2,1,0:T(8,128)(2,1)S(1)} %get-tuple-element.721), channel_id=1, source_target_pairs={{0,1},{1,2},{2,3},{3,4},{4,5},{5,6},{6,7},{7,8},{8,9},{9,10},{10,1... | collective-permute-start | bytes 1572872 | tf_op jit(solution)/shard_map/while/body/eval_jaxpr/ppermute | solution.py:10
  92.9 17.0 %collective-permute-start = (bf16[8,128,256]{2,1,0:T(8,128)(2,1)S(1)}, bf16[8,128,256]{2,1,0:T(8,128)(2,1)S(1)}, u32[]{:S(2)}, u32[]{:S(2)}) collective-permute-start(bf16[8,128,256]{2,1,0:T(8,128)(2,1)S(1)} %get-tuple-element.721), channel_id=1, source_target_pairs={{0,1},{1,2},{2,3},{3,4},{4,5},{5,6},{6,7},{7,8},{8,9},{9,10},{10,1... | collective-permute-start | bytes 1572872 | tf_op jit(solution)/shard_map/while/body/eval_jaxpr/ppermute | solution.py:10
  159.4 12.2 %collective-permute-start = (bf16[8,128,256]{2,1,0:T(8,128)(2,1)S(1)}, bf16[8,128,256]{2,1,0:T(8,128)(2,1)S(1)}, u32[]{:S(2)}, u32[]{:S(2)}) collective-permute-start(bf16[8,128,256]{2,1,0:T(8,128)(2,1)S(1)} %get-tuple-element.721), channel_id=1, source_target_pairs={{0,1},{1,2},{2,3},{3,4},{4,5},{5,6},{6,7},{7,8},{8,9},{9,10},{10,1... | collective-permute-start | bytes 1572872 | tf_op jit(solution)/shard_map/while/body/eval_jaxpr/ppermute | solution.py:10
  180.0 12.2 %collective-permute-start = (bf16[8,128,256]{2,1,0:T(8,128)(2,1)S(1)}, bf16[8,128,256]{2,1,0:T(8,128)(2,1)S(1)}, u32[]{:S(2)}, u32[]{:S(2)}) collective-permute-start(bf16[8,128,256]{2,1,0:T(8,128)(2,1)S(1)} %get-tuple-element.721), channel_id=1, source_target_pairs={{0,1},{1,2},{2,3},{3,4},{4,5},{5,6},{6,7},{7,8},{8,9},{9,10},{10,1... | collective-permute-start | bytes 1572872 | tf_op jit(solution)/shard_map/while/body/eval_jaxpr/ppermute | solution.py:10
  262.3 12.2 %collective-permute-start = (bf16[8,128,256]{2,1,0:T(8,128)(2,1)S(1)}, bf16[8,128,256]{2,1,0:T(8,128)(2,1)S(1)}, u32[]{:S(2)}, u32[]{:S(2)}) collective-permute-start(bf16[8,128,256]{2,1,0:T(8,128)(2,1)S(1)} %get-tuple-element.721), channel_id=1, source_target_pairs={{0,1},{1,2},{2,3},{3,4},{4,5},{5,6},{6,7},{7,8},{8,9},{9,10},{10,1... | collective-permute-start | bytes 1572872 | tf_op jit(solution)/shard_map/while/body/eval_jaxpr/ppermute | solution.py:10
  282.9 12.2 %collective-permute-start = (bf16[8,128,256]{2,1,0:T(8,128)(2,1)S(1)}, bf16[8,128,256]{2,1,0:T(8,128)(2,1)S(1)}, u32[]{:S(2)}, u32[]{:S(2)}) collective-permute-start(bf16[8,128,256]{2,1,0:T(8,128)(2,1)S(1)} %get-tuple-element.721), channel_id=1, source_target_pairs={{0,1},{1,2},{2,3},{3,4},{4,5},{5,6},{6,7},{7,8},{8,9},{9,10},{10,1... | collective-permute-start | bytes 1572872 | tf_op jit(solution)/shard_map/while/body/eval_jaxpr/ppermute | solution.py:10
  377.1 36.4 %all-to-all-start.1 = ((bf16[8,4,128,256]{3,2,1,0:T(8,128)(2,1)}), bf16[8,4,128,256]{3,2,1,0:T(8,128)(2,1)S(1)}, u32[]{:S(2)}, u32[]{:S(2)}) async-start(bf16[8,4,128,256]{3,2,1,0:T(8,128)(2,1)} %copy.60), calls=%async_computation.1 | async-start | bytes 4194304 | tf_op jit(solution)/shard_map/all_to_all | solution.py:129
  380.8 656.6 %all-gather.3.cloned.1.call-start = ((), (), s32[]{:S(2)}) async-start(), calls=%async_computation.2 | async-start | bytes 33816576 | tf_op jit(solution)/shard_map/all_gather | solution.py:145
  417.6 13.4 %collective-permute-start.1 = (f32[8,128,256]{2,0,1:T(8,128)}, f32[8,128,256]{2,0,1:T(8,128)}, u32[]{:S(2)}, u32[]{:S(2)}) collective-permute-start(f32[8,128,256]{2,0,1:T(8,128)} %get-tuple-element.757), channel_id=1, source_target_pairs={{0,1},{1,2},{2,3},{3,4},{4,5},{5,6},{6,7},{7,8},{8,9},{9,10},{10,1... | collective-permute-start | bytes 3145736 | tf_op jit(solution)/shard_map/while/body/eval_jaxpr/ppermute | solution.py:10
  437.6 18.1 %collective-permute-start.1 = (f32[8,128,256]{2,0,1:T(8,128)}, f32[8,128,256]{2,0,1:T(8,128)}, u32[]{:S(2)}, u32[]{:S(2)}) collective-permute-start(f32[8,128,256]{2,0,1:T(8,128)} %get-tuple-element.757), channel_id=1, source_target_pairs={{0,1},{1,2},{2,3},{3,4},{4,5},{5,6},{6,7},{7,8},{8,9},{9,10},{10,1... | collective-permute-start | bytes 3145736 | tf_op jit(solution)/shard_map/while/body/eval_jaxpr/ppermute | solution.py:10
  462.3 18.2 %collective-permute-start.1 = (f32[8,128,256]{2,0,1:T(8,128)}, f32[8,128,256]{2,0,1:T(8,128)}, u32[]{:S(2)}, u32[]{:S(2)}) collective-permute-start(f32[8,128,256]{2,0,1:T(8,128)} %get-tuple-element.757), channel_id=1, source_target_pairs={{0,1},{1,2},{2,3},{3,4},{4,5},{5,6},{6,7},{7,8},{8,9},{9,10},{10,1... | collective-permute-start | bytes 3145736 | tf_op jit(solution)/shard_map/while/body/eval_jaxpr/ppermute | solution.py:10
  487.0 18.2 %collective-permute-start.1 = (f32[8,128,256]{2,0,1:T(8,128)}, f32[8,128,256]{2,0,1:T(8,128)}, u32[]{:S(2)}, u32[]{:S(2)}) collective-permute-start(f32[8,128,256]{2,0,1:T(8,128)} %get-tuple-element.757), channel_id=1, source_target_pairs={{0,1},{1,2},{2,3},{3,4},{4,5},{5,6},{6,7},{7,8},{8,9},{9,10},{10,1... | collective-permute-start | bytes 3145736 | tf_op jit(solution)/shard_map/while/body/eval_jaxpr/ppermute | solution.py:10
  511.7 18.2 %collective-permute-start.1 = (f32[8,128,256]{2,0,1:T(8,128)}, f32[8,128,256]{2,0,1:T(8,128)}, u32[]{:S(2)}, u32[]{:S(2)}) collective-permute-start(f32[8,128,256]{2,0,1:T(8,128)} %get-tuple-element.757), channel_id=1, source_target_pairs={{0,1},{1,2},{2,3},{3,4},{4,5},{5,6},{6,7},{7,8},{8,9},{9,10},{10,1... | collective-permute-start | bytes 3145736 | tf_op jit(solution)/shard_map/while/body/eval_jaxpr/ppermute | solution.py:10
  536.4 18.2 %collective-permute-start.1 = (f32[8,128,256]{2,0,1:T(8,128)}, f32[8,128,256]{2,0,1:T(8,128)}, u32[]{:S(2)}, u32[]{:S(2)}) collective-permute-start(f32[8,128,256]{2,0,1:T(8,128)} %get-tuple-element.757), channel_id=1, source_target_pairs={{0,1},{1,2},{2,3},{3,4},{4,5},{5,6},{6,7},{7,8},{8,9},{9,10},{10,1... | collective-permute-start | bytes 3145736 | tf_op jit(solution)/shard_map/while/body/eval_jaxpr/ppermute | solution.py:10
  561.2 18.2 %collective-permute-start.1 = (f32[8,128,256]{2,0,1:T(8,128)}, f32[8,128,256]{2,0,1:T(8,128)}, u32[]{:S(2)}, u32[]{:S(2)}) collective-permute-start(f32[8,128,256]{2,0,1:T(8,128)} %get-tuple-element.757), channel_id=1, source_target_pairs={{0,1},{1,2},{2,3},{3,4},{4,5},{5,6},{6,7},{7,8},{8,9},{9,10},{10,1... | collective-permute-start | bytes 3145736 | tf_op jit(solution)/shard_map/while/body/eval_jaxpr/ppermute | solution.py:10
  585.9 18.2 %collective-permute-start.1 = (f32[8,128,256]{2,0,1:T(8,128)}, f32[8,128,256]{2,0,1:T(8,128)}, u32[]{:S(2)}, u32[]{:S(2)}) collective-permute-start(f32[8,128,256]{2,0,1:T(8,128)} %get-tuple-element.757), channel_id=1, source_target_pairs={{0,1},{1,2},{2,3},{3,4},{4,5},{5,6},{6,7},{7,8},{8,9},{9,10},{10,1... | collective-permute-start | bytes 3145736 | tf_op jit(solution)/shard_map/while/body/eval_jaxpr/ppermute | solution.py:10
  610.6 18.2 %collective-permute-start.1 = (f32[8,128,256]{2,0,1:T(8,128)}, f32[8,128,256]{2,0,1:T(8,128)}, u32[]{:S(2)}, u32[]{:S(2)}) collective-permute-start(f32[8,128,256]{2,0,1:T(8,128)} %get-tuple-element.757), channel_id=1, source_target_pairs={{0,1},{1,2},{2,3},{3,4},{4,5},{5,6},{6,7},{7,8},{8,9},{9,10},{10,1... | collective-permute-start | bytes 3145736 | tf_op jit(solution)/shard_map/while/body/eval_jaxpr/ppermute | solution.py:10
  635.3 18.2 %collective-permute-start.1 = (f32[8,128,256]{2,0,1:T(8,128)}, f32[8,128,256]{2,0,1:T(8,128)}, u32[]{:S(2)}, u32[]{:S(2)}) collective-permute-start(f32[8,128,256]{2,0,1:T(8,128)} %get-tuple-element.757), channel_id=1, source_target_pairs={{0,1},{1,2},{2,3},{3,4},{4,5},{5,6},{6,7},{7,8},{8,9},{9,10},{10,1... | collective-permute-start | bytes 3145736 | tf_op jit(solution)/shard_map/while/body/eval_jaxpr/ppermute | solution.py:10
  660.1 18.2 %collective-permute-start.1 = (f32[8,128,256]{2,0,1:T(8,128)}, f32[8,128,256]{2,0,1:T(8,128)}, u32[]{:S(2)}, u32[]{:S(2)}) collective-permute-start(f32[8,128,256]{2,0,1:T(8,128)} %get-tuple-element.757), channel_id=1, source_target_pairs={{0,1},{1,2},{2,3},{3,4},{4,5},{5,6},{6,7},{7,8},{8,9},{9,10},{10,1... | collective-permute-start | bytes 3145736 | tf_op jit(solution)/shard_map/while/body/eval_jaxpr/ppermute | solution.py:10
  684.8 18.2 %collective-permute-start.1 = (f32[8,128,256]{2,0,1:T(8,128)}, f32[8,128,256]{2,0,1:T(8,128)}, u32[]{:S(2)}, u32[]{:S(2)}) collective-permute-start(f32[8,128,256]{2,0,1:T(8,128)} %get-tuple-element.757), channel_id=1, source_target_pairs={{0,1},{1,2},{2,3},{3,4},{4,5},{5,6},{6,7},{7,8},{8,9},{9,10},{10,1... | collective-permute-start | bytes 3145736 | tf_op jit(solution)/shard_map/while/body/eval_jaxpr/ppermute | solution.py:10
  709.5 18.2 %collective-permute-start.1 = (f32[8,128,256]{2,0,1:T(8,128)}, f32[8,128,256]{2,0,1:T(8,128)}, u32[]{:S(2)}, u32[]{:S(2)}) collective-permute-start(f32[8,128,256]{2,0,1:T(8,128)} %get-tuple-element.757), channel_id=1, source_target_pairs={{0,1},{1,2},{2,3},{3,4},{4,5},{5,6},{6,7},{7,8},{8,9},{9,10},{10,1... | collective-permute-start | bytes 3145736 | tf_op jit(solution)/shard_map/while/body/eval_jaxpr/ppermute | solution.py:10
  734.2 18.2 %collective-permute-start.1 = (f32[8,128,256]{2,0,1:T(8,128)}, f32[8,128,256]{2,0,1:T(8,128)}, u32[]{:S(2)}, u32[]{:S(2)}) collective-permute-start(f32[8,128,256]{2,0,1:T(8,128)} %get-tuple-element.757), channel_id=1, source_target_pairs={{0,1},{1,2},{2,3},{3,4},{4,5},{5,6},{6,7},{7,8},{8,9},{9,10},{10,1... | collective-permute-start | bytes 3145736 | tf_op jit(solution)/shard_map/while/body/eval_jaxpr/ppermute | solution.py:10
  759.0 18.2 %collective-permute-start.1 = (f32[8,128,256]{2,0,1:T(8,128)}, f32[8,128,256]{2,0,1:T(8,128)}, u32[]{:S(2)}, u32[]{:S(2)}) collective-permute-start(f32[8,128,256]{2,0,1:T(8,128)} %get-tuple-element.757), channel_id=1, source_target_pairs={{0,1},{1,2},{2,3},{3,4},{4,5},{5,6},{6,7},{7,8},{8,9},{9,10},{10,1... | collective-permute-start | bytes 3145736 | tf_op jit(solution)/shard_map/while/body/eval_jaxpr/ppermute | solution.py:10
  (49 other events, 563.4 us)
Sparse Core Ops, SparseCore 0:
  787.8 249.5 all-gather.2
